TPU v7x, 32 devices: a whole 2x2x4 slice. The times are simulated.
32 devices in a mesh: dp: 4 (over y, core), expert: 8 (over z, x).
Axes of the slice: x: 2, y: 2, z: 4, core: 2. Of those that a mesh axis runs over, the one named last changes fastest.
Arguments:
- tokens: bfloat16 [1024, 7168], P('expert', 'dp'), may hold values from -6 to 6
- routes: int32 [1024, 8], P('expert'), may hold values from 0 to 31, all different within a row; in each aligned block of 128 rows (0 to 127, 128 to 255, ...) at most 64 rows name the same one
- route_weight: float32 [1024, 8], P('expert'), may hold values from 0.1 to 1
- gate_first: bfloat16 [32, 64, 112, 32], P('expert', 'dp'), may hold values from -0.5 to 0.5
- up_first: bfloat16 [32, 64, 112, 32], P('expert', 'dp'), may hold values from -0.5 to 0.5
- gate_second: bfloat16 [32, 32, 64, 64], P('expert', 'dp'), may hold values from -0.75 to 0.75
- up_second: bfloat16 [32, 32, 64, 64], P('expert', 'dp'), may hold values from -0.75 to 0.75
- down_first: bfloat16 [32, 32, 64, 64], P('expert', 'dp'), may hold values from -0.75 to 0.75
- down_second: bfloat16 [32, 64, 32, 112], P('expert', 'dp'), may hold values from -1 to 1
Outputs:
- moe_output: bfloat16 [1024, 7168], P('expert', 'dp')
- expert_load: float32 [32], P('expert')
Inputs may be any that keep to these rules, and one draw needn't show every extreme that they name: `routes`: each row names 8 different experts. Within each device's aligned block of 128 rows no expert is named by more than 64 rows, and in some block an expert is named by exactly 64 rows.
All inputs are finite; a program needn't handle non-finite values.
Results may differ from a plain program's by a relative error of at most 0.0076.
Values may be sent and summed in bfloat16 or wider, within the bound.
A program may use at most 64 MiB of HBM per device.

v0:
```python
import functools

import jax
import jax.numpy as jnp
from jax import lax
from jax.experimental import pallas as pl
from jax.experimental.pallas import tpu as pltpu
from jax.sharding import PartitionSpec as P

F32 = jnp.float32
BF16 = jnp.bfloat16
MESH = pl.DeviceIdType.MESH


def shards(
    tokens,
    routes,
    route_weight,
    gate_first,
    up_first,
    gate_second,
    up_second,
    down_first,
    down_second,
):
    tok_rows, width_here = tokens.shape
    top_k = routes.shape[1]
    groups = lax.axis_size("expert")
    dp_count = lax.axis_size("dp")
    per_dev, blocks_here, block_width, rank_size = gate_first.shape
    rank_here = gate_second.shape[1]
    block_count = gate_second.shape[2]
    experts = per_dev * groups
    capacity = 2 * tok_rows * top_k // experts
    flat_routes = routes.reshape(-1)
    pair_count = flat_routes.shape[0]
    one_hot = (flat_routes[:, None] == jnp.arange(experts, dtype=jnp.int32)[None, :]).astype(
        jnp.int32
    )
    earlier = jnp.cumsum(one_hot, axis=0) - one_hot
    position = jnp.sum(earlier * one_hot, axis=1)
    counts = jnp.sum(one_hot, axis=0)
    slot_index = flat_routes * capacity + position
    pair_token = jnp.arange(pair_count, dtype=jnp.int32) // top_k
    slot_token = jnp.full((experts * capacity,), tok_rows, jnp.int32).at[slot_index].set(pair_token)
    outgoing = jnp.take(tokens, slot_token, axis=0, mode="fill", fill_value=0).reshape(
        groups, per_dev, capacity, width_here
    )
    gate_wide = gate_second.reshape(per_dev, rank_here, dp_count, blocks_here, block_count)
    up_wide = up_second.reshape(per_dev, rank_here, dp_count, blocks_here, block_count)
    down_wide = down_second.reshape(per_dev, blocks_here, dp_count, rank_here, block_width)
    received = lax.all_to_all(outgoing, "expert", split_axis=0, concat_axis=0, tiled=True)
    sources = received.shape[0]
    local = received.shape[1]
    slots = received.shape[2]
    split_rows = received.reshape(sources, local, slots, blocks_here, block_width)
    gate_low = jnp.einsum(
        "aesbf,ebfr->rbeas", split_rows, gate_first, preferred_element_type=jnp.float32
    )
    up_low = jnp.einsum(
        "aesbf,ebfr->rbeas", split_rows, up_first, preferred_element_type=jnp.float32
    )
    layout = (dp_count, rank_here, blocks_here, local, sources, slots)
    gate_mixed = lax.all_to_all(
        gate_low.astype(jnp.bfloat16).reshape(layout), "dp", split_axis=0, concat_axis=0, tiled=True
    )
    up_mixed = lax.all_to_all(
        up_low.astype(jnp.bfloat16).reshape(layout), "dp", split_axis=0, concat_axis=0, tiled=True
    )
    gate_high = jnp.einsum(
        "qcjeas,ecqjm->ecmas", gate_mixed, gate_wide, preferred_element_type=jnp.float32
    )
    up_high = jnp.einsum(
        "qcjeas,ecqjm->ecmas", up_mixed, up_wide, preferred_element_type=jnp.float32
    )
    activated = (jax.nn.silu(gate_high) * up_high).astype(jnp.bfloat16)
    down_low = jnp.einsum(
        "ecmas,ecmn->ecnas", activated, down_first, preferred_element_type=jnp.float32
    )
    down_split = down_low.astype(jnp.bfloat16).reshape(
        local, rank_here, dp_count, blocks_here, sources, slots
    )
    down_mixed = lax.all_to_all(down_split, "dp", split_axis=2, concat_axis=2, tiled=True)
    expert_out = jnp.einsum(
        "ecqjas,ejqcf->aesjf", down_mixed, down_wide, preferred_element_type=jnp.float32
    )
    result = expert_out.astype(jnp.bfloat16).reshape(sources, local, slots, width_here)
    totals = lax.psum(counts, "expert")
    own_counts = lax.dynamic_slice_in_dim(
        totals, lax.axis_index("expert") * per_dev, per_dev
    ).astype(jnp.float32)
    returned = lax.all_to_all(result, "expert", split_axis=0, concat_axis=0, tiled=True).reshape(
        experts * capacity, width_here
    )
    picked = jnp.take(returned, slot_index, axis=0).astype(jnp.float32)
    weighted = picked * route_weight.reshape(-1)[:, None]
    moe_output = jnp.sum(weighted.reshape(tok_rows, top_k, width_here), axis=1).astype(jnp.bfloat16)
    expert_load = own_counts * experts / (tok_rows * groups * top_k)
    return (moe_output, expert_load)


def xor(a, b, count):
    total, bit = 0, 1
    while bit < count:
        total = total + bit * ((a // bit + b // bit) % 2)
        bit *= 2
    return total


def dot(a, b):
    return jnp.dot(a, b, preferred_element_type=F32)


def ones_at(shape, row_to_column):
    lead = shape[:-1]
    target = row_to_column(*[lax.broadcasted_iota(jnp.int32, shape, d) for d in range(len(lead))])
    column = lax.broadcasted_iota(jnp.int32, shape, len(lead))
    hit = jnp.where(column == target, F32(1), F32(0))
    return hit.reshape(-1, shape[-1]).astype(BF16)


def expert_kernel(
    sizes,
    tok, routes, shares_in, gf, uf, gs, df, ds,
    out, load,
    tok_all, routes_all, shares_all, gf2, uf2, gs2, df2, ds2,
    w1, w2, w3, w4, wide, rows, low_out, low_in, down_out, down_in,
    combine, made, summed, z_out, z_in, counts, counts_in,
    gather_s, gather_r, weight_s, weight_r, low_s, low_r, down_s, down_r,
    local_s, count_s, z_s, z_r,
):
    groups, dp, top_k, cap, rank_here, block_count = sizes
    per_dev, blocks, rank, width = gf.shape
    tok_rows, features = tok.shape
    experts = per_dev * groups
    half = blocks // 2
    half_width = half * width
    chunk = 2 * rank_here * half
    pieces = 2 * dp
    hidden = rank_here * block_count
    nz = groups // 2
    total_steps = 2 * nz
    d = lax.axis_index("dp")
    g = lax.axis_index("expert")
    z, x = g // 2, g % 2
    partner = (d, z * 2 + (1 - x))

    def at_dp(r):
        return (xor(d, r, dp), g)

    def at_z(k):
        return (d, xor(z, k, nz) * 2 + x)

    def remote(src, dst, send, recv, to):
        return pltpu.make_async_remote_copy(
            src_ref=src, dst_ref=dst, send_sem=send, recv_sem=recv,
            device_id=to, device_id_type=MESH,
        )

    barrier = pltpu.get_barrier_semaphore()
    peers = [at_dp(r) for r in range(1, dp)] + [partner] + [at_z(k) for k in range(1, nz)]
    for peer in peers:
        pl.semaphore_signal(barrier, inc=1, device_id=peer, device_id_type=MESH)
    pl.semaphore_wait(barrier, len(peers))

    def gather(k):
        pairs = ((routes, routes_all), (shares_in, shares_all), (tok, tok_all))
        return [
            remote(src, dst.at[k], gather_s.at[n, k], gather_r.at[n, k], at_z(k))
            for n, (src, dst) in enumerate(pairs)
        ]

    held = (gf, uf, gs, df, ds)
    swapped = (gf2, uf2, gs2, df2, ds2)

    def swap(n):
        return remote(held[n], swapped[n], weight_s.at[n], weight_r.at[n], partner)

    for k in range(1, nz):
        for copy in gather(k):
            copy.start()
    for n in range(len(held)):
        swap(n).start()
    tok_all[0] = tok[...]
    routes_all[0] = routes[...]
    shares_all[0] = shares_in[...]
    counts[...] = jnp.zeros_like(counts)

    def spread_first(gate, up):
        @pl.loop(0, blocks)
        def _(b):
            j = b % half
            place = ones_at(
                (2, dp, rank_here, dp * chunk),
                lambda side, q, c: q * chunk + side * (chunk // 2) + c * half + j,
            )
            for e in range(per_dev):
                both = jnp.concatenate([gate[e, b], up[e, b]], axis=0)
                w1[e, b] = lax.dot_general(
                    both, place, (((0,), (0,)), ((), ())), preferred_element_type=F32
                ).astype(BF16)

    def spread_middle(second, third):
        wide[...] = jnp.zeros_like(wide)

        @pl.loop(0, per_dev)
        def _(e):
            for side in range(2):
                for c in range(rank_here):
                    lane = (c * block_count) % 128
                    place = ones_at(
                        (2, block_count, 128),
                        lambda s, r: jnp.where(s == side, r + lane, -1),
                    )
                    value = dot(second[e, c], place)
                    row = side * (chunk // 2) + c * half
                    start = side * hidden + c * block_count - lane
                    wide[:, row : row + half, start : start + 128] = value.reshape(
                        pieces, half, 128
                    )
            for piece in range(pieces):
                w2[e, piece] = wide[piece].astype(BF16)

        @pl.loop(0, rank_here)
        def _(c):
            pairs = rank_here // 2
            place = ones_at(
                (2, block_count, hidden),
                lambda s, r: jnp.where(s == c // pairs, r * rank_here + c, -1),
            )
            value = dot(third[:, c % pairs].reshape(-1, 2 * block_count), place)
            w3[:, c] = value.astype(BF16).reshape(per_dev, block_count, hidden)

    def spread_last(fourth):
        wide[...] = jnp.zeros_like(wide)

        @pl.loop(0, per_dev)
        def _(e):
            for n in range(blocks):
                h = n // half
                offset = (n % half) * width
                lane = offset % 128
                span = -(-(lane + width) // 128) * 128
                value = dot(fourth[e, n], ones_at((width, span), lambda r: r + lane))
                wide[
                    h * dp : (h + 1) * dp,
                    n * rank_here : (n + 1) * rank_here,
                    offset - lane : offset - lane + span,
                ] = value.reshape(dp, rank_here, span)
            for q in range(dp):
                for h in range(2):
                    w4[e, q, :, h * half_width : (h + 1) * half_width] = wide[
                        h * dp + q, :, :half_width
                    ].astype(BF16)

    def place_of(i):
        turn = i // nz
        return turn, (i % nz) * (1 - turn) + (nz - 1 - i % nz) * turn

    def low_copy(i, r):
        return remote(
            low_out.at[i % 2, xor(d, r, dp)], low_in.at[i, d],
            low_s.at[i % 2, r], low_r.at[i, r], at_dp(r),
        )

    def down_copy(i, r):
        return remote(
            down_out.at[i % 2, xor(d, r, dp)], down_in.at[i, d],
            down_s.at[i % 2, r], down_r.at[i, r], at_dp(r),
        )

    def low_local(i):
        return pltpu.make_async_copy(low_out.at[i % 2, d], low_in.at[i, d], local_s.at[0])

    def down_local(i):
        return pltpu.make_async_copy(down_out.at[i % 2, d], down_in.at[i, d], local_s.at[1])

    crossing = list(range(dp - 1, 0, -1))

    def stage_a(i):
        turn, k = place_of(i)

        @pl.when((turn == 0) & (k > 0))
        def _():
            for copy in gather(k):
                copy.wait_recv()

        @pl.when(i >= 2)
        def _():
            for r in crossing:
                low_copy(i, r).wait_send()

        base = (z * 2 + (x + turn) % 2) * per_dev
        named_rows, weights = routes_all[k], shares_all[k]
        line = lax.broadcasted_iota(jnp.int32, (8, tok_rows), 0)
        hits = jnp.zeros((8, tok_rows), F32)
        shares = []
        for e in range(per_dev):
            named = named_rows == base + e
            hit = jnp.max(jnp.where(named, F32(1), F32(0)), axis=0, keepdims=True)
            hits = hits + jnp.where(line == e, hit, F32(0))
            shares.append(jnp.sum(jnp.where(named, weights, F32(0)), axis=0, keepdims=True))
        counts[turn] += hits
        before = lax.broadcasted_iota(jnp.int32, (tok_rows, tok_rows), 0)
        after = lax.broadcasted_iota(jnp.int32, (tok_rows, tok_rows), 1)
        ahead = jnp.where(before < after, F32(1), F32(0)).astype(BF16)
        position = dot(hits.astype(BF16), ahead)
        position = jnp.where(hits > 0, position, F32(-1)).astype(jnp.int32)
        slot_row = lax.broadcasted_iota(jnp.int32, (cap, tok_rows), 0)
        pick, mix = [], []
        for e in range(per_dev):
            chosen = slot_row == position[e : e + 1]
            pick.append(jnp.where(chosen, F32(1), F32(0)))
            mix.append(jnp.where(chosen, shares[e], F32(0)))
        pick = jnp.concatenate(pick, axis=0).astype(BF16)
        combine[i] = jnp.concatenate(mix, axis=0).T.astype(BF16)
        rows[...] = dot(pick, tok_all[k]).astype(BF16)
        for e in range(per_dev):
            span = slice(e * cap, (e + 1) * cap)
            for h in range(2):
                weight = w1[e, h * half : (h + 1) * half].reshape(half_width, dp * chunk)
                low = dot(rows[span, h * half_width : (h + 1) * half_width], weight).astype(BF16)
                for q in range(dp):
                    low_out[i % 2, q, h, span, :] = low[:, q * chunk : (q + 1) * chunk]
        for r in crossing:
            low_copy(i, r).start()
        low_local(i).start()
        low_local(i).wait()

    def stage_b(i):
        for r in crossing:
            low_copy(i, r).wait_recv()

        @pl.when(i >= 2)
        def _():
            for r in crossing:
                down_copy(i, r).wait_send()

        for e in range(per_dev):
            span = slice(e * cap, (e + 1) * cap)
            low = jnp.concatenate(
                [low_in[i, p, h, span, :] for p in range(dp) for h in range(2)], axis=1
            )
            high = dot(low, w2[e].reshape(pieces * chunk, 2 * hidden))
            gate, up = high[:, :hidden], high[:, hidden:]
            activated = (gate / (1 + jnp.exp(-gate)) * up).astype(BF16)
            down = dot(activated, w3[e].reshape(hidden, hidden)).astype(BF16)
            for p in range(dp):
                down_out[i % 2, p, span, :] = down[:, p * chunk : (p + 1) * chunk]
        for r in crossing:
            down_copy(i, r).start()
        down_local(i).start()
        down_local(i).wait()

    def z_part(k):
        return remote(z_out.at[k], z_in.at[k], z_s.at[k], z_r.at[k], at_z(k))

    def stage_c(i):
        turn, k = place_of(i)
        for r in crossing:
            down_copy(i, r).wait_recv()
        for e in range(per_dev):
            span = slice(e * cap, (e + 1) * cap)
            down = jnp.concatenate([down_in[i, q, span, :] for q in range(dp)], axis=1)
            made[span, :] = dot(down, w4[e].reshape(dp * chunk, features)).astype(BF16)
        part = dot(combine[i], made[...])

        @pl.when(turn == 0)
        def _():
            summed[k] = part

        @pl.when((turn == 1) & (k == 0))
        def _():
            summed[k] += part

        @pl.when((turn == 1) & (k > 0))
        def _():
            z_out[k] = (summed[k] + part).astype(BF16)
            z_part(k).start()

    count_copy = remote(counts.at[1], counts_in, count_s.at[0], count_s.at[1], partner)

    spread_first(gf, uf)

    @pl.loop(0, total_steps + 2)
    def _(step):
        @pl.when(step == nz)
        def _():
            swap(0).wait_recv()
            swap(1).wait_recv()
            spread_first(gf2, uf2)

        @pl.when(step < total_steps)
        def _():
            stage_a(step)

        @pl.when(step == 0)
        def _():
            spread_middle(gs, df)
            spread_last(ds)

        @pl.when(step == total_steps)
        def _():
            count_copy.start()

        @pl.when(step == nz + 1)
        def _():
            swap(2).wait_recv()
            swap(3).wait_recv()
            spread_middle(gs2, df2)

        @pl.when((step >= 1) & (step <= total_steps))
        def _():
            stage_b(step - 1)

        @pl.when(step == nz + 2)
        def _():
            swap(4).wait_recv()
            spread_last(ds2)

        @pl.when(step >= 2)
        def _():
            stage_c(step - 2)

    count_copy.wait()
    ones = jnp.ones((8, tok_rows), BF16)
    held_rows = lax.dot_general(
        ones, (counts[0] + counts_in[...]).astype(BF16),
        (((1,), (1,)), ((), ())), preferred_element_type=F32,
    )
    load[...] = held_rows[:1, :per_dev] * experts / (tok_rows * groups * top_k)

    total = summed[0]
    for k in range(1, nz):
        z_part(k).wait_recv()
        total += z_in[k].astype(F32)
    out[...] = total.astype(BF16)

    for k in range(1, nz):
        for copy in gather(k):
            copy.wait_send()
        z_part(k).wait_send()
    for n in range(len(held)):
        swap(n).wait_send()
    for i in (total_steps - 2, total_steps - 1):
        for r in crossing:
            low_copy(i, r).wait_send()
            down_copy(i, r).wait_send()


def fused(
    tokens, routes, route_weight,
    gate_first, up_first, gate_second, up_second, down_first, down_second,
):
    tok_rows, features = tokens.shape
    top_k = routes.shape[1]
    groups = lax.axis_size("expert")
    dp = lax.axis_size("dp")
    per_dev, blocks, width, rank = gate_first.shape
    rank_here, block_count = gate_second.shape[1:3]
    experts = per_dev * groups
    cap = 2 * tok_rows * top_k // experts
    nz = groups // 2
    steps = 2 * nz
    chunk = 2 * rank_here * (blocks // 2)
    hidden = rank_here * block_count
    slots = per_dev * cap
    pairs = rank_here // 2
    factors = (
        gate_first.swapaxes(2, 3),
        up_first.swapaxes(2, 3),
        jnp.concatenate([gate_second, up_second], axis=3),
        jnp.concatenate([down_first[:, :pairs], down_first[:, pairs:]], axis=3),
        down_second,
    )
    vmem = pl.BlockSpec(memory_space=pltpu.VMEM)
    dma = pltpu.SemaphoreType.DMA
    out, load = pl.pallas_call(
        functools.partial(expert_kernel, (groups, dp, top_k, cap, rank_here, block_count)),
        out_shape=(
            jax.ShapeDtypeStruct((tok_rows, features), BF16),
            jax.ShapeDtypeStruct((1, per_dev), F32),
        ),
        in_specs=[vmem] * 8,
        out_specs=(vmem, vmem),
        scratch_shapes=[
            pltpu.VMEM((nz, tok_rows, features), BF16),
            pltpu.VMEM((nz, top_k, tok_rows), jnp.int32),
            pltpu.VMEM((nz, top_k, tok_rows), F32),
            *[pltpu.VMEM(factor.shape, BF16) for factor in factors],
            pltpu.VMEM((per_dev, blocks, width, dp * chunk), BF16),
            pltpu.VMEM((per_dev, 2 * dp, chunk, 2 * hidden), BF16),
            pltpu.VMEM((per_dev, rank_here, block_count, hidden), BF16),
            pltpu.VMEM((per_dev, dp, chunk, features), BF16),
            pltpu.VMEM((2 * dp, chunk, 2 * hidden), F32),
            pltpu.VMEM((slots, features), BF16),
            pltpu.VMEM((2, dp, 2, slots, chunk), BF16),
            pltpu.VMEM((steps, dp, 2, slots, chunk), BF16),
            pltpu.VMEM((2, dp, slots, chunk), BF16),
            pltpu.VMEM((steps, dp, slots, chunk), BF16),
            pltpu.VMEM((steps, tok_rows, slots), BF16),
            pltpu.VMEM((slots, features), BF16),
            pltpu.VMEM((nz, tok_rows, features), F32),
            pltpu.VMEM((nz, tok_rows, features), BF16),
            pltpu.VMEM((nz, tok_rows, features), BF16),
            pltpu.VMEM((2, 8, tok_rows), F32),
            pltpu.VMEM((8, tok_rows), F32),
            dma((3, nz)), dma((3, nz)), dma((5,)), dma((5,)),
            dma((2, dp)), dma((steps, dp)), dma((2, dp)), dma((steps, dp)),
            dma((2,)), dma((2,)), dma((nz,)), dma((nz,)),
        ],
        compiler_params=pltpu.CompilerParams(
            collective_id=0, has_side_effects=True, vmem_limit_bytes=67043328
        ),
    )(tokens, routes.T, route_weight.T, *factors)
    return (out, load.reshape(per_dev))


def chosen_plan(tokens, routes, route_weight, *weights):
    groups = lax.axis_size("expert")
    dp = lax.axis_size("dp")
    blocks, width = weights[0].shape[1:3]
    rank_here, block_count = weights[2].shape[1:3]
    tiled = (
        tokens.shape[0] % 128 == 0
        and 2 * rank_here * (blocks // 2) == 128
        and rank_here == 8
        and weights[0].shape[0] <= 8
        and blocks // 2 == 8
        and block_count == 2 * dp * 8
        and (blocks // 2 * width) % 128 == 0
    )
    powers = groups & (groups - 1) == 0 and dp & (dp - 1) == 0
    if groups <= 2 * routes.shape[1] and groups >= 4 and dp >= 2 and powers and tiled:
        return fused(tokens, routes, route_weight, *weights)
    return shards(tokens, routes, route_weight, *weights)


def solution(mesh):
    return jax.shard_map(
        chosen_plan,
        mesh=mesh,
        in_specs=(
            P("expert", "dp"),
            P("expert", None),
            P("expert", None),
            P("expert", "dp", None, None),
            P("expert", "dp", None, None),
            P("expert", "dp", None, None),
            P("expert", "dp", None, None),
            P("expert", "dp", None, None),
            P("expert", "dp", None, None),
        ),
        out_specs=(P("expert", "dp"), P("expert")),
        check_vma=False,
    )
```

profile of v0, /device:TPU:0, one launch (start us, length us, event | category | flops | bytes accessed | tf_op | source)
XLA Modules:
  0.0 129.9 jit_solution(17969350881516084892)
XLA Ops:
  0.6 0.0 copy-start.1
  0.6 1.1 fusion
  1.8 0.0 copy-start
  1.8 0.9 pad_maximum_fusion.1.df
  2.7 0.0 copy-done.1
  2.7 0.2 copy-done
  2.8 1.1 pad_maximum_fusion.gs
  3.9 123.6 %shard_map.104 = (bf16[128,1792]{1,0:T(8,128)(2,1)}, f32[1,4]{1,0:T(1,128)}) custom-call(bf16[128,1792]{1,0:T(8,128)(2,1)} %tok.1, s32[8,128]{1,0:T(8,128)} %bitcast.7, f32[8,128]{1,0:T(8,128)} %bitcast.8, bf16[4,16,32,112]{3,2,1,0:T(8,128)(2,1)} %bitcast.5, bf16[4,16,32,112]{3,2,1,0:T(8,128)(2,1)} %bitcast.6, bf16[4,8,64,128]{3,2,1,0:T(8,128)(2,1)} %pad_maximum_fusion.gs, ...), custom_call_target="tpu_custom_call" | custom-call | tf_op jit(solution)/shard_map/pallas_call | solution.py:478
  127.6 0.0 copy-start.2
  127.6 1.8 %copy.13 = bf16[128,1792]{1,0:T(8,128)(2,1)} copy(bf16[128,1792]{1,0:T(8,128)(2,1)} %get-tuple-element.10) | data formatting | bytes 917504
  129.4 0.0 copy-done.2
  129.4 0.5 copy.14
Async XLA Ops:
  0.6 2.0 %copy-start.1 = (bf16[4,8,64,64]{3,2,1,0:T(8,128)(2,1)S(1)}, bf16[4,8,64,64]{3,2,1,0:T(8,128)(2,1)}, u32[]{:S(2)}) copy-start(bf16[4,8,64,64]{3,2,1,0:T(8,128)(2,1)} %param.14) | copy-start | bytes 786436
  1.8 1.1 copy-start
  127.6 1.8 %copy-start.2 = (f32[1,4]{1,0:T(1,128)S(1)}, f32[1,4]{1,0:T(1,128)}, u32[]{:S(2)}) copy-start(f32[1,4]{1,0:T(1,128)} %get-tuple-element.5) | copy-start | bytes 52
where the time goes:
time: 130 us
  Pallas kernels  124 us (95%)
  local copies, waits for them, and re-layouts  3.66 us (3%)
  other arithmetic  1.95 us (2%)
    pallas_call x1, Pallas kernels, fused(): pl.pallas_call(functools.partial(expert_kernel, (groups, dp, top_k, cap,...  124 us

commit v1 on v0

v1 whole, which is shorter than its diff:
```python
import functools

import jax
import jax.numpy as jnp
from jax import lax
from jax.experimental import pallas as pl
from jax.experimental.pallas import tpu as pltpu
from jax.sharding import PartitionSpec as P

F32 = jnp.float32
BF16 = jnp.bfloat16
MESH = pl.DeviceIdType.MESH
LAGS = (3, 6)


def shards(
    tokens,
    routes,
    route_weight,
    gate_first,
    up_first,
    gate_second,
    up_second,
    down_first,
    down_second,
):
    tok_rows, width_here = tokens.shape
    top_k = routes.shape[1]
    groups = lax.axis_size("expert")
    dp_count = lax.axis_size("dp")
    per_dev, blocks_here, block_width, rank_size = gate_first.shape
    rank_here = gate_second.shape[1]
    block_count = gate_second.shape[2]
    experts = per_dev * groups
    capacity = 2 * tok_rows * top_k // experts
    flat_routes = routes.reshape(-1)
    pair_count = flat_routes.shape[0]
    one_hot = (flat_routes[:, None] == jnp.arange(experts, dtype=jnp.int32)[None, :]).astype(
        jnp.int32
    )
    earlier = jnp.cumsum(one_hot, axis=0) - one_hot
    position = jnp.sum(earlier * one_hot, axis=1)
    counts = jnp.sum(one_hot, axis=0)
    slot_index = flat_routes * capacity + position
    pair_token = jnp.arange(pair_count, dtype=jnp.int32) // top_k
    slot_token = jnp.full((experts * capacity,), tok_rows, jnp.int32).at[slot_index].set(pair_token)
    outgoing = jnp.take(tokens, slot_token, axis=0, mode="fill", fill_value=0).reshape(
        groups, per_dev, capacity, width_here
    )
    gate_wide = gate_second.reshape(per_dev, rank_here, dp_count, blocks_here, block_count)
    up_wide = up_second.reshape(per_dev, rank_here, dp_count, blocks_here, block_count)
    down_wide = down_second.reshape(per_dev, blocks_here, dp_count, rank_here, block_width)
    received = lax.all_to_all(outgoing, "expert", split_axis=0, concat_axis=0, tiled=True)
    sources = received.shape[0]
    local = received.shape[1]
    slots = received.shape[2]
    split_rows = received.reshape(sources, local, slots, blocks_here, block_width)
    gate_low = jnp.einsum(
        "aesbf,ebfr->rbeas", split_rows, gate_first, preferred_element_type=jnp.float32
    )
    up_low = jnp.einsum(
        "aesbf,ebfr->rbeas", split_rows, up_first, preferred_element_type=jnp.float32
    )
    layout = (dp_count, rank_here, blocks_here, local, sources, slots)
    gate_mixed = lax.all_to_all(
        gate_low.astype(jnp.bfloat16).reshape(layout), "dp", split_axis=0, concat_axis=0, tiled=True
    )
    up_mixed = lax.all_to_all(
        up_low.astype(jnp.bfloat16).reshape(layout), "dp", split_axis=0, concat_axis=0, tiled=True
    )
    gate_high = jnp.einsum(
        "qcjeas,ecqjm->ecmas", gate_mixed, gate_wide, preferred_element_type=jnp.float32
    )
    up_high = jnp.einsum(
        "qcjeas,ecqjm->ecmas", up_mixed, up_wide, preferred_element_type=jnp.float32
    )
    activated = (jax.nn.silu(gate_high) * up_high).astype(jnp.bfloat16)
    down_low = jnp.einsum(
        "ecmas,ecmn->ecnas", activated, down_first, preferred_element_type=jnp.float32
    )
    down_split = down_low.astype(jnp.bfloat16).reshape(
        local, rank_here, dp_count, blocks_here, sources, slots
    )
    down_mixed = lax.all_to_all(down_split, "dp", split_axis=2, concat_axis=2, tiled=True)
    expert_out = jnp.einsum(
        "ecqjas,ejqcf->aesjf", down_mixed, down_wide, preferred_element_type=jnp.float32
    )
    result = expert_out.astype(jnp.bfloat16).reshape(sources, local, slots, width_here)
    totals = lax.psum(counts, "expert")
    own_counts = lax.dynamic_slice_in_dim(
        totals, lax.axis_index("expert") * per_dev, per_dev
    ).astype(jnp.float32)
    returned = lax.all_to_all(result, "expert", split_axis=0, concat_axis=0, tiled=True).reshape(
        experts * capacity, width_here
    )
    picked = jnp.take(returned, slot_index, axis=0).astype(jnp.float32)
    weighted = picked * route_weight.reshape(-1)[:, None]
    moe_output = jnp.sum(weighted.reshape(tok_rows, top_k, width_here), axis=1).astype(jnp.bfloat16)
    expert_load = own_counts * experts / (tok_rows * groups * top_k)
    return (moe_output, expert_load)


def xor(a, b, count):
    total, bit = 0, 1
    while bit < count:
        total = total + bit * ((a // bit + b // bit) % 2)
        bit *= 2
    return total


def dot(a, b):
    return jnp.dot(a, b, preferred_element_type=F32)


def one_hot(hit):
    return jnp.where(hit, F32(1), F32(0)).astype(BF16)


def swap_groups(a, b, size):
    lane = lax.broadcasted_iota(jnp.int32, a.shape, len(a.shape) - 1)
    even = (lane // size) % 2 == 0
    axis = len(a.shape) - 1
    first = jnp.where(even, a, pltpu.roll(b, size, axis))
    second = jnp.where(even, pltpu.roll(a, 128 - size, axis), b)
    return first, second


def expert_kernel(
    sizes,
    tok, routes, shares_in, gf, uf, gs_in, us_in, df_in, ds,
    out, load,
    tok_all, routes_all, shares_all, gs, df, gf2, uf2, gs2, df2, ds2,
    w1, w2, w3, w4, place1, place3, rows,
    low_out, low_in, down_out, down_in,
    combine, made, summed, z_out, z_in, counts, counts_in,
    gather_s, gather_r, weight_s, weight_r, low_s, low_r, down_s, down_r,
    local_low, local_down, count_s, z_s, z_r,
):
    groups, dp, top_k, cap, rank_here, block_count = sizes
    per_dev, blocks, rank, width = gf.shape
    tok_rows, features = tok.shape
    experts = per_dev * groups
    half = blocks // 2
    half_width = half * width
    chunk = 2 * rank_here * half
    hidden = rank_here * block_count
    pairs = rank_here // 2
    quad = pairs * block_count
    nz = groups // 2
    steps = 2 * nz
    units = steps * per_dev
    ring = low_out.shape[0]
    lag_b, lag_c = LAGS
    d = lax.axis_index("dp")
    g = lax.axis_index("expert")
    z, x = g // 2, g % 2
    partner = (d, z * 2 + (1 - x))
    inner = (z >= 1) & (z < nz - 1)

    def at_dp(r):
        return (xor(d, r, dp), g)

    def at_z(k):
        return (d, xor(z, k, nz) * 2 + x)

    def remote(src, dst, send, recv, to):
        return pltpu.make_async_remote_copy(
            src_ref=src, dst_ref=dst, send_sem=send, recv_sem=recv,
            device_id=to, device_id_type=MESH,
        )

    barrier = pltpu.get_barrier_semaphore()
    peers = [at_dp(r) for r in range(1, dp)] + [partner] + [at_z(k) for k in range(1, nz)]
    for peer in peers:
        pl.semaphore_signal(barrier, inc=1, device_id=peer, device_id_type=MESH)
    pl.semaphore_wait(barrier, len(peers))

    own = ((routes, routes_all), (shares_in, shares_all), (tok, tok_all))

    def gather(link, source, to, slot):
        return [
            remote(
                src if source == 0 else dst.at[source], dst.at[slot],
                gather_s.at[n, link], gather_r.at[n, slot], at_z(to),
            )
            for n, (src, dst) in enumerate(own)
        ]

    sends = (gather(0, 0, 1, 1), gather(1, 0, 3, 3))
    relays = (gather(2, 1, 3, 2), gather(3, 3, 1, 2), gather(4, 2, 1, 3))

    def arrived(slot):
        for copy in gather(0, 0, 1, slot):
            copy.wait_recv()

    held = (gf, uf, gs, df, ds)
    swapped = (gf2, uf2, gs2, df2, ds2)

    def swap(n):
        return remote(held[n], swapped[n], weight_s.at[n], weight_r.at[n], partner)

    for copy in sends[0]:
        copy.start()

    @pl.when(inner)
    def _():
        for copy in sends[1]:
            copy.start()

    swap(0).start()
    swap(1).start()
    tok_all[0] = tok[...]
    routes_all[0] = routes[...]
    shares_all[0] = shares_in[...]
    counts[...] = jnp.zeros_like(counts)

    row1 = lax.broadcasted_iota(jnp.int32, (2 * rank, dp * chunk), 0)
    col1 = lax.broadcasted_iota(jnp.int32, (2 * rank, dp * chunk), 1)
    side1, rest1 = row1 // rank, row1 % rank
    base1 = (rest1 // rank_here) * chunk + side1 * (chunk // 2) + (rest1 % rank_here) * half
    for j in range(half):
        place1[j] = one_hot(col1 == base1 + j)

    def spread_first(e, turn, gate, up):
        for b in range(blocks):
            both = jnp.concatenate([gate[e, b], up[e, b]], axis=0)
            w1[turn, e, b] = lax.dot_general(
                both, place1[b % half], (((0,), (0,)), ((), ())), preferred_element_type=F32
            ).astype(BF16)

    def spread_middle(e, turn, second, third):
        lane = lax.broadcasted_iota(jnp.int32, (block_count, 128), 1)
        low_half = lane < block_count
        nothing = jnp.zeros((block_count // half, half, 128), F32)
        for part in range(rank_here // pairs):
            tiles = ([], [])
            for c in range(pairs):
                value = second[e, part * pairs + c].astype(F32)
                turned = pltpu.roll(value, block_count, 1)
                for side in range(2):
                    if c % 2 == 0:
                        kept = jnp.where(low_half, value if side == 0 else turned, F32(0))
                    else:
                        kept = jnp.where(low_half, F32(0), turned if side == 0 else value)
                    kept = kept.reshape(block_count // half, half, 128)
                    spots = [nothing] * (quad // 128)
                    spots[c // 2] = kept
                    tiles[side].append(jnp.concatenate(spots, axis=2))
            for side in range(2):
                tile = jnp.stack(tiles[side], axis=1).reshape(quad, quad)
                w2[turn, e, side * (rank_here // pairs) + part] = tile.astype(BF16)
        for c in range(rank_here):
            value = dot(third[e, c % pairs], place3[c])
            w3[turn, e, c * block_count : (c + 1) * block_count] = value.astype(BF16)

    def spread_last(e, turn, fourth):
        lane = lax.broadcasted_iota(jnp.int32, (rank, 128), 1)
        nothing = jnp.zeros((dp, rank_here, 128), F32)
        for h in range(2):
            stripes = []
            for n in range(half):
                value = fourth[e, h * half + n].astype(F32)
                value = jnp.concatenate(
                    [value, jnp.zeros((rank, 128 - width), F32)], axis=1
                )
                spot, shift = (n * width) // 128, (n * width) % 128
                spots = [nothing] * (half_width // 128)
                if shift == 0:
                    spots[spot] = value.reshape(dp, rank_here, 128)
                else:
                    turned = pltpu.roll(value, shift, 1)
                    spots[spot] = jnp.where(lane >= shift, turned, F32(0)).reshape(
                        dp, rank_here, 128
                    )
                    if shift + width > 128:
                        spots[spot + 1] = jnp.where(lane < shift, turned, F32(0)).reshape(
                            dp, rank_here, 128
                        )
                stripes.append(jnp.concatenate(spots, axis=2))
            tile = jnp.stack(stripes, axis=1).reshape(dp * chunk // 2, half_width)
            w4[turn, e, h] = tile.astype(BF16)

    def place_of(i):
        turn = i // nz
        return turn, (i % nz) * (1 - turn) + (nz - 1 - i % nz) * turn

    def low_copy(u, r):
        return remote(
            low_out.at[u % ring, xor(d, r, dp)], low_in.at[u, d],
            low_s.at[u % ring, r], low_r.at[u, r], at_dp(r),
        )

    def down_copy(u, r):
        return remote(
            down_out.at[u % ring, xor(d, r, dp)], down_in.at[u, d],
            down_s.at[u % ring, r], down_r.at[u, r], at_dp(r),
        )

    def low_local(u):
        return pltpu.make_async_copy(
            low_out.at[u % ring, d], low_in.at[u, d], local_low.at[u % ring]
        )

    def down_local(u):
        return pltpu.make_async_copy(
            down_out.at[u % ring, d], down_in.at[u, d], local_down.at[u % ring]
        )

    crossing = list(range(dp - 1, 0, -1))

    def pick_rows(i):
        turn, k = place_of(i)

        @pl.when(i == 1)
        def _():
            arrived(1)

            @pl.when(inner)
            def _():
                for copy in relays[0]:
                    copy.start()
                arrived(3)
                for copy in relays[1]:
                    copy.start()

        @pl.when(i == 2)
        def _():
            arrived(2)

            @pl.when(inner)
            def _():
                for copy in relays[2]:
                    copy.start()

        @pl.when((i == 3) & jnp.logical_not(inner))
        def _():
            arrived(3)

        base = (z * 2 + (x + turn) % 2) * per_dev
        named_rows, weights = routes_all[k], shares_all[k]
        line = lax.broadcasted_iota(jnp.int32, (8, tok_rows), 0)
        hits = jnp.zeros((8, tok_rows), F32)
        shares = []
        for e in range(per_dev):
            named = named_rows == base + e
            hit = jnp.max(jnp.where(named, F32(1), F32(0)), axis=0, keepdims=True)
            hits = hits + jnp.where(line == e, hit, F32(0))
            shares.append(jnp.sum(jnp.where(named, weights, F32(0)), axis=0, keepdims=True))
        counts[turn] += hits
        before = lax.broadcasted_iota(jnp.int32, (tok_rows, tok_rows), 0)
        after = lax.broadcasted_iota(jnp.int32, (tok_rows, tok_rows), 1)
        position = dot(hits.astype(BF16), one_hot(before < after))
        position = jnp.where(hits > 0, position, F32(-1)).astype(jnp.int32)
        slot_row = lax.broadcasted_iota(jnp.int32, (cap, tok_rows), 0)
        pick, mix = [], []
        for e in range(per_dev):
            chosen = slot_row == position[e : e + 1]
            pick.append(jnp.where(chosen, F32(1), F32(0)))
            mix.append(jnp.where(chosen, shares[e], F32(0)))
        pick = jnp.concatenate(pick, axis=0).astype(BF16)
        combine[i] = jnp.concatenate(mix, axis=0).T.astype(BF16)
        rows[...] = dot(pick, tok_all[k]).astype(BF16).reshape(per_dev, cap, features)

    def stage_a(u):
        i, e = u // per_dev, u % per_dev
        turn = i // nz

        @pl.when(u >= ring)
        def _():
            for r in crossing:
                low_copy(u - ring, r).wait_send()

        @pl.when(e == 0)
        def _():
            pick_rows(i)

        for h in range(2):
            weight = w1[turn, e, h * half : (h + 1) * half].reshape(half_width, dp * chunk)
            low = dot(rows[e, :, h * half_width : (h + 1) * half_width], weight).astype(BF16)
            for q in range(dp):
                low_out[u % ring, q, h] = low[:, q * chunk : (q + 1) * chunk]
        for r in crossing:
            low_copy(u, r).start()
        low_local(u).start()

    def stage_b(u):
        i, e = u // per_dev, u % per_dev
        turn = i // nz
        low_local(u).wait()
        for r in crossing:
            low_copy(u, r).wait_recv()

        @pl.when(u >= ring)
        def _():
            for r in crossing:
                down_copy(u - ring, r).wait_send()

        groups_of = []
        for lead in range(0, dp, 2):
            a, b, c_, d_ = [low_in[u, p, h] for p in (lead, lead + 1) for h in range(2)]
            a, c_ = swap_groups(a, c_, 64)
            b, d_ = swap_groups(b, d_, 64)
            a, b = swap_groups(a, b, 32)
            c_, d_ = swap_groups(c_, d_, 32)
            groups_of.append((a, b, c_, d_))
        high = [
            dot(jnp.concatenate([group[n] for group in groups_of], axis=1), w2[turn, e, n])
            for n in range(4)
        ]
        gate = jnp.concatenate(high[:2], axis=1)
        up = jnp.concatenate(high[2:], axis=1)
        activated = (gate / (1 + jnp.exp(-gate)) * up).astype(BF16)
        down = dot(activated, w3[turn, e]).astype(BF16)
        for p in range(dp):
            down_out[u % ring, p] = down[:, p * chunk : (p + 1) * chunk]
        for r in crossing:
            down_copy(u, r).start()
        down_local(u).start()

    def z_part(n, slot, to, h):
        return remote(z_out.at[n, h], z_in.at[slot, h], z_s.at[n, h], z_r.at[slot, h], at_z(to))

    def z_send(n, slot, to, h, value):
        z_out[n, h] = value.astype(BF16)
        z_part(n, slot, to, h).start()

    def z_wait(slot, h):
        z_part(0, slot, 1, h).wait_recv()

    def pass_far(h):
        z_wait(3, h)
        z_send(1, 4, 3, h, summed[2, h] + z_in[3, h].astype(F32))

    def pass_near(h):
        z_wait(4, h)
        z_send(0, 0, 1, h, summed[1, h] + z_in[4, h].astype(F32))

    def pass_across(h):
        z_wait(2, h)
        z_send(2, 5, 3, h, summed[3, h] + z_in[2, h].astype(F32))

    def stage_c(u):
        i, e = u // per_dev, u % per_dev
        turn, k = place_of(i)
        down_local(u).wait()
        for r in crossing:
            down_copy(u, r).wait_recv()
        pieces = [down_in[u, q] for q in range(dp)]
        low_a, high_a = swap_groups(pieces[0], pieces[1], 64)
        low_b, high_b = swap_groups(pieces[2], pieces[3], 64)
        for h, value in enumerate(((low_a, low_b), (high_a, high_b))):
            result = dot(jnp.concatenate(value, axis=1), w4[turn, e, h])
            made[h, e] = result.astype(BF16)

        @pl.when(e == per_dev - 1)
        def _():
            for h in range(2):
                part = dot(combine[i], made[h].reshape(per_dev * cap, half_width))

                @pl.when(turn == 0)
                def _():
                    summed[k, h] = part

                @pl.when((turn == 1) & ((k == 0) | inner))
                def _():
                    summed[k, h] += part

                for n in range(1, nz):

                    @pl.when((turn == 1) & (k == n) & jnp.logical_not(inner))
                    def _():
                        z_send(n - 1, n, 1, h, summed[n, h] + part)

    count_copy = remote(counts.at[1], counts_in, count_s.at[0], count_s.at[1], partner)

    for e in range(per_dev):
        for c in range(rank_here):
            gs[e, c] = jnp.concatenate([gs_in[e, c], us_in[e, c]], axis=1)
        for c in range(pairs):
            df[e, c] = jnp.concatenate([df_in[e, c], df_in[e, c + pairs]], axis=1)
    for n in range(2, 5):
        swap(n).start()
    row3 = lax.broadcasted_iota(jnp.int32, (2 * block_count, hidden), 0)
    col3 = lax.broadcasted_iota(jnp.int32, (2 * block_count, hidden), 1)
    for c in range(rank_here):
        offset = (c // pairs) * block_count
        hit = (row3 >= offset) & (row3 < offset + block_count)
        place3[c] = one_hot(hit & (col3 == (row3 - offset) * rank_here + c))

    far_steps = nz * per_dev
    first_at, middle_at = far_steps - per_dev - 1, far_steps + 1
    last_at = far_steps + lag_c

    @pl.loop(0, units + lag_c)
    def _(t):
        @pl.when(t < per_dev)
        def _():
            spread_first(t, 0, gf, uf)

        @pl.when((t >= first_at) & (t < first_at + per_dev))
        def _():
            @pl.when(t == first_at)
            def _():
                swap(0).wait_recv()
                swap(1).wait_recv()

            spread_first(t - first_at, 1, gf2, uf2)

        @pl.when(t < units)
        def _():
            stage_a(t)

        @pl.when((t >= lag_b) & (t < lag_b + per_dev))
        def _():
            spread_middle(t - lag_b, 0, gs, df)

        @pl.when((t >= middle_at) & (t < middle_at + per_dev))
        def _():
            @pl.when(t == middle_at)
            def _():
                swap(2).wait_recv()
                swap(3).wait_recv()

            spread_middle(t - middle_at, 1, gs2, df2)

        @pl.when((t >= lag_b) & (t < units + lag_b))
        def _():
            stage_b(t - lag_b)

        @pl.when((t >= lag_c) & (t < lag_c + per_dev))
        def _():
            spread_last(t - lag_c, 0, ds)

        @pl.when((t >= last_at) & (t < last_at + per_dev))
        def _():
            @pl.when(t == last_at)
            def _():
                swap(4).wait_recv()

            spread_last(t - last_at, 1, ds2)

        @pl.when(t >= lag_c)
        def _():
            stage_c(t - lag_c)

        @pl.when(t == units)
        def _():
            count_copy.start()

        done_far = (steps - 2) * per_dev + lag_c - 1
        for h in range(2):

            @pl.when(inner & (t == done_far + h))
            def _():
                pass_far(h)

        @pl.when(inner & (t == done_far + per_dev))
        def _():
            pass_across(0)

        @pl.when(inner & (t == done_far + per_dev + 1))
        def _():
            pass_near(0)

    @pl.when(inner)
    def _():
        pass_near(1)
        pass_across(1)

    count_copy.wait()
    ones = jnp.ones((8, tok_rows), BF16)
    held_rows = lax.dot_general(
        ones, (counts[0] + counts_in[...]).astype(BF16),
        (((1,), (1,)), ((), ())), preferred_element_type=F32,
    )
    load[...] = held_rows[:1, :per_dev] * experts / (tok_rows * groups * top_k)

    for h in range(2):
        span = slice(h * half_width, (h + 1) * half_width)

        @pl.when(inner)
        def _():
            z_wait(1, h)
            z_wait(5, h)
            both = z_in[1, h].astype(F32) + z_in[5, h].astype(F32)
            out[:, span] = (summed[0, h] + both).astype(BF16)

        @pl.when(jnp.logical_not(inner))
        def _():
            z_wait(0, h)
            out[:, span] = (summed[0, h] + z_in[0, h].astype(F32)).astype(BF16)

    for copy in sends[0]:
        copy.wait_send()

    @pl.when(inner)
    def _():
        for copies in (sends[1],) + relays:
            for copy in copies:
                copy.wait_send()

    for n in range(3):
        for h in range(2):
            z_part(n, 0, 1, h).wait_send()
    for n in range(len(held)):
        swap(n).wait_send()

    @pl.loop(units - ring, units)
    def _(u):
        for r in crossing:
            low_copy(u, r).wait_send()
            down_copy(u, r).wait_send()


def fused(
    tokens, routes, route_weight,
    gate_first, up_first, gate_second, up_second, down_first, down_second,
):
    tok_rows, features = tokens.shape
    top_k = routes.shape[1]
    groups = lax.axis_size("expert")
    dp = lax.axis_size("dp")
    per_dev, blocks, width, rank = gate_first.shape
    rank_here, block_count = gate_second.shape[1:3]
    experts = per_dev * groups
    cap = 2 * tok_rows * top_k // experts
    nz = groups // 2
    steps = 2 * nz
    units = steps * per_dev
    ring = 8
    half = blocks // 2
    chunk = 2 * rank_here * half
    hidden = rank_here * block_count
    slots = per_dev * cap
    pairs = rank_here // 2
    quad = pairs * block_count
    half_width = half * width
    first = (per_dev, blocks, rank, width)
    joined = (per_dev, rank_here, block_count, 2 * block_count)
    paired = (per_dev, pairs, block_count, 2 * block_count)
    last = down_second.shape
    vmem = pl.BlockSpec(memory_space=pltpu.VMEM)
    dma = pltpu.SemaphoreType.DMA
    out, load = pl.pallas_call(
        functools.partial(expert_kernel, (groups, dp, top_k, cap, rank_here, block_count)),
        out_shape=(
            jax.ShapeDtypeStruct((tok_rows, features), BF16),
            jax.ShapeDtypeStruct((1, per_dev), F32),
        ),
        in_specs=[vmem] * 9,
        out_specs=(vmem, vmem),
        scratch_shapes=[
            pltpu.VMEM((nz, tok_rows, features), BF16),
            pltpu.VMEM((nz, top_k, tok_rows), jnp.int32),
            pltpu.VMEM((nz, top_k, tok_rows), F32),
            *[pltpu.VMEM(s, BF16) for s in (joined, paired)],
            *[pltpu.VMEM(s, BF16) for s in (first, first, joined, paired, last)],
            pltpu.VMEM((2, per_dev, blocks, width, dp * chunk), BF16),
            pltpu.VMEM((2, per_dev, 4, quad, quad), BF16),
            pltpu.VMEM((2, per_dev, hidden, hidden), BF16),
            pltpu.VMEM((2, per_dev, 2, dp * chunk // 2, half_width), BF16),
            pltpu.VMEM((half, 2 * rank, dp * chunk), BF16),
            pltpu.VMEM((rank_here, 2 * block_count, hidden), BF16),
            pltpu.VMEM((per_dev, cap, features), BF16),
            pltpu.VMEM((ring, dp, 2, cap, chunk), BF16),
            pltpu.VMEM((units, dp, 2, cap, chunk), BF16),
            pltpu.VMEM((ring, dp, cap, chunk), BF16),
            pltpu.VMEM((units, dp, cap, chunk), BF16),
            pltpu.VMEM((steps, tok_rows, slots), BF16),
            pltpu.VMEM((2, per_dev, cap, half_width), BF16),
            pltpu.VMEM((nz, 2, tok_rows, half_width), F32),
            pltpu.VMEM((3, 2, tok_rows, half_width), BF16),
            pltpu.VMEM((6, 2, tok_rows, half_width), BF16),
            pltpu.VMEM((2, 8, tok_rows), F32),
            pltpu.VMEM((8, tok_rows), F32),
            dma((3, 5)), dma((3, nz)), dma((5,)), dma((5,)),
            dma((ring, dp)), dma((units, dp)), dma((ring, dp)), dma((units, dp)),
            dma((ring,)), dma((ring,)), dma((2,)), dma((3, 2)), dma((6, 2)),
        ],
        compiler_params=pltpu.CompilerParams(
            collective_id=0, has_side_effects=True, vmem_limit_bytes=67043328
        ),
    )(
        tokens, routes.T, route_weight.T, gate_first.swapaxes(2, 3), up_first.swapaxes(2, 3),
        gate_second, up_second, down_first, down_second,
    )
    return (out, load.reshape(per_dev))


def chosen_plan(tokens, routes, route_weight, *weights):
    groups = lax.axis_size("expert")
    dp = lax.axis_size("dp")
    blocks, width = weights[0].shape[1:3]
    rank_here, block_count = weights[2].shape[1:3]
    tiled = (
        tokens.shape[0] % 128 == 0
        and 2 * rank_here * (blocks // 2) == 128
        and rank_here == 8
        and weights[0].shape[0] <= 8
        and blocks // 2 == 8
        and block_count == 2 * dp * 8
        and (blocks // 2 * width) % 128 == 0
    )
    powers = groups & (groups - 1) == 0 and dp & (dp - 1) == 0
    if groups <= 2 * routes.shape[1] and groups == 8 and dp == 4 and powers and tiled:
        return fused(tokens, routes, route_weight, *weights)
    return shards(tokens, routes, route_weight, *weights)


def solution(mesh):
    return jax.shard_map(
        chosen_plan,
        mesh=mesh,
        in_specs=(
            P("expert", "dp"),
            P("expert", None),
            P("expert", None),
            P("expert", "dp", None, None),
            P("expert", "dp", None, None),
            P("expert", "dp", None, None),
            P("expert", "dp", None, None),
            P("expert", "dp", None, None),
            P("expert", "dp", None, None),
        ),
        out_specs=(P("expert", "dp"), P("expert")),
        check_vma=False,
    )
```

time: 130 us -> 106 us (0.82)
  Pallas kernels: 124 us -> 102 us
  other arithmetic: 1.95 us -> 0 us
  local copies, waits for them, and re-layouts: 3.66 us -> 2.33 us
    pallas_call x1, Pallas kernels: 124 us -> 102 us  [fused(): pl.pallas_call(functools.partial(expert_kernel, (groups, dp, top_k, cap,...]
    concatenate x2 -> x0, other arithmetic: 1.95 us -> none  [the longest x1 1.09 us: fused(): jnp.concatenate([gate_second, up_second], axis=3)]
where the time goes in v1:
time: 106 us; the launch traced here: 105 us
  Pallas kernels  102 us (96%)
  local copies, waits for them, and re-layouts  2.33 us (2%)
    pallas_call x1, Pallas kernels, fused(): pl.pallas_call(functools.partial(expert_kernel, (groups, dp, top_k, cap,...  102 us
    unnamed x4, local copies, waits for them, and re-layouts  2.33 us

profile of v1, /device:TPU:0, one launch (start us, length us, event | category | flops | bytes accessed | tf_op | source)
XLA Modules:
  0.0 105.4 jit_solution(281596574749129983)
XLA Ops:
  0.6 102.4 %shard_map.104 = (bf16[128,1792]{1,0:T(8,128)(2,1)}, f32[1,4]{1,0:T(1,128)}) custom-call(bf16[128,1792]{1,0:T(8,128)(2,1)} %tok.1, s32[8,128]{1,0:T(8,128)} %bitcast.7, f32[8,128]{1,0:T(8,128)} %bitcast.8, bf16[4,16,32,112]{3,2,1,0:T(8,128)(2,1)} %bitcast.5, bf16[4,16,32,112]{3,2,1,0:T(8,128)(2,1)} %bitcast.6, bf16[4,8,64,64]{3,2,1,0:T(8,128)(2,1)} %gs_in.1, ...), custom_call_target="tpu_custom_call" | custom-call | tf_op jit(solution)/shard_map/pallas_call | solution.py:644
  103.1 0.0 copy-start
  103.1 1.8 %copy.13 = bf16[128,1792]{1,0:T(8,128)(2,1)} copy(bf16[128,1792]{1,0:T(8,128)(2,1)} %get-tuple-element.8) | data formatting | bytes 917504
  104.9 0.0 copy-done
  104.9 0.5 copy.14
Async XLA Ops:
  103.1 1.8 %copy-start = (f32[1,4]{1,0:T(1,128)S(1)}, f32[1,4]{1,0:T(1,128)}, u32[]{:S(2)}) copy-start(f32[1,4]{1,0:T(1,128)} %get-tuple-element.5) | copy-start | bytes 52

commit v2 on v1

--- a/solution.py
+++ b/solution.py
@@ -10,7 +10,7 @@
 F32 = jnp.float32
 BF16 = jnp.bfloat16
 MESH = pl.DeviceIdType.MESH
-LAGS = (3, 6)
+LAGS = (2, 4)
 
 
 def shards(
@@ -127,14 +127,15 @@
 
 def expert_kernel(
     sizes,
-    tok, routes, shares_in, gf, uf, gs_in, us_in, df_in, ds,
+    tok, routes, shares_in, gf_arg, uf_arg, gs_arg, us_arg, df_arg, ds_arg,
     out, load,
-    tok_all, routes_all, shares_all, gs, df, gf2, uf2, gs2, df2, ds2,
+    tok_all, routes_all, shares_all, gf, uf, gs_in, us_in, df_in, ds,
+    gs, df, gf2, uf2, gs2, df2, ds2,
     w1, w2, w3, w4, place1, place3, rows,
     low_out, low_in, down_out, down_in,
     combine, made, summed, z_out, z_in, counts, counts_in,
     gather_s, gather_r, weight_s, weight_r, low_s, low_r, down_s, down_r,
-    local_low, local_down, count_s, z_s, z_r,
+    local_low, local_down, load_s, count_s, z_s, z_r,
 ):
     groups, dp, top_k, cap, rank_here, block_count = sizes
     per_dev, blocks, rank, width = gf.shape
@@ -170,27 +171,49 @@
         )
 
     barrier = pltpu.get_barrier_semaphore()
-    peers = [at_dp(r) for r in range(1, dp)] + [partner] + [at_z(k) for k in range(1, nz)]
+    peers = [at_dp(r) for r in range(1, dp)] + [partner, at_z(1)]
+
+    def greet(peer):
+        pl.semaphore_signal(barrier, inc=1, device_id=peer, device_id_type=MESH)
+
     for peer in peers:
-        pl.semaphore_signal(barrier, inc=1, device_id=peer, device_id_type=MESH)
-    pl.semaphore_wait(barrier, len(peers))
-
-    own = ((routes, routes_all), (shares_in, shares_all), (tok, tok_all))
-
-    def gather(link, source, to, slot):
+        greet(peer)
+
+    @pl.when(inner)
+    def _():
+        greet(at_z(3))
+
+    inputs = (
+        (gf_arg, gf), (uf_arg, uf), (routes, routes_all.at[0]), (shares_in, shares_all.at[0]),
+        (tok, tok_all.at[0]), (gs_arg, gs_in), (us_arg, us_in), (df_arg, df_in), (ds_arg, ds),
+    )
+    loads = [
+        pltpu.make_async_copy(src, dst, load_s.at[n]) for n, (src, dst) in enumerate(inputs)
+    ]
+    for copy in loads:
+        copy.start()
+
+    part_rows = tok_rows // 2
+
+    def gather(link, source, to, slot, h):
+        rows_of = pl.ds(h * part_rows, part_rows)
+        pairs_of = [(tok_all.at[source, rows_of], tok_all.at[slot, rows_of])]
+        if h == 0:
+            pairs_of += [(ref.at[source], ref.at[slot]) for ref in (routes_all, shares_all)]
         return [
-            remote(
-                src if source == 0 else dst.at[source], dst.at[slot],
-                gather_s.at[n, link], gather_r.at[n, slot], at_z(to),
-            )
-            for n, (src, dst) in enumerate(own)
+            remote(src, dst, gather_s.at[n + 3 * h, link], gather_r.at[n + 3 * h, slot], at_z(to))
+            for n, (src, dst) in enumerate(pairs_of)
         ]
 
-    sends = (gather(0, 0, 1, 1), gather(1, 0, 3, 3))
-    relays = (gather(2, 1, 3, 2), gather(3, 3, 1, 2), gather(4, 2, 1, 3))
-
-    def arrived(slot):
-        for copy in gather(0, 0, 1, slot):
+    def begin(copies):
+        for copy in copies:
+            copy.start()
+
+    sends = ((0, 0, 1, 1), (1, 0, 3, 3))
+    relays = ((2, 1, 3, 2), (3, 3, 1, 2), (4, 2, 1, 3))
+
+    def arrived(slot, h):
+        for copy in gather(0, 0, 1, slot, h):
             copy.wait_recv()
 
     held = (gf, uf, gs, df, ds)
@@ -199,27 +222,14 @@
     def swap(n):
         return remote(held[n], swapped[n], weight_s.at[n], weight_r.at[n], partner)
 
-    for copy in sends[0]:
-        copy.start()
-
-    @pl.when(inner)
-    def _():
-        for copy in sends[1]:
-            copy.start()
-
-    swap(0).start()
-    swap(1).start()
-    tok_all[0] = tok[...]
-    routes_all[0] = routes[...]
-    shares_all[0] = shares_in[...]
     counts[...] = jnp.zeros_like(counts)
-
-    row1 = lax.broadcasted_iota(jnp.int32, (2 * rank, dp * chunk), 0)
-    col1 = lax.broadcasted_iota(jnp.int32, (2 * rank, dp * chunk), 1)
-    side1, rest1 = row1 // rank, row1 % rank
-    base1 = (rest1 // rank_here) * chunk + side1 * (chunk // 2) + (rest1 % rank_here) * half
-    for j in range(half):
-        place1[j] = one_hot(col1 == base1 + j)
+    def make_places():
+        row1 = lax.broadcasted_iota(jnp.int32, (2 * rank, dp * chunk), 0)
+        col1 = lax.broadcasted_iota(jnp.int32, (2 * rank, dp * chunk), 1)
+        side1, rest1 = row1 // rank, row1 % rank
+        base1 = (rest1 // rank_here) * chunk + side1 * (chunk // 2) + (rest1 % rank_here) * half
+        for j in range(half):
+            place1[j] = one_hot(col1 == base1 + j)
 
     def spread_first(e, turn, gate, up):
         for b in range(blocks):
@@ -308,34 +318,38 @@
 
     crossing = list(range(dp - 1, 0, -1))
 
+    def pass_tokens(h):
+        arrived(1, h)
+
+        @pl.when(inner)
+        def _():
+            begin(gather(*relays[0], h))
+            arrived(3, h)
+            begin(gather(*relays[1], h))
+
+    def pass_last(h):
+        arrived(2, h)
+
+        @pl.when(inner)
+        def _():
+            begin(gather(*relays[2], h))
+
+    def meet(i):
+        @pl.when(i == 1)
+        def _():
+            pass_tokens(1)
+
+        @pl.when(i == 2)
+        def _():
+            pass_last(1)
+
+        @pl.when((i == 3) & jnp.logical_not(inner))
+        def _():
+            arrived(3, 0)
+            arrived(3, 1)
+
     def pick_rows(i):
         turn, k = place_of(i)
-
-        @pl.when(i == 1)
-        def _():
-            arrived(1)
-
-            @pl.when(inner)
-            def _():
-                for copy in relays[0]:
-                    copy.start()
-                arrived(3)
-                for copy in relays[1]:
-                    copy.start()
-
-        @pl.when(i == 2)
-        def _():
-            arrived(2)
-
-            @pl.when(inner)
-            def _():
-                for copy in relays[2]:
-                    copy.start()
-
-        @pl.when((i == 3) & jnp.logical_not(inner))
-        def _():
-            arrived(3)
-
         base = (z * 2 + (x + turn) % 2) * per_dev
         named_rows, weights = routes_all[k], shares_all[k]
         line = lax.broadcasted_iota(jnp.int32, (8, tok_rows), 0)
@@ -361,27 +375,33 @@
         combine[i] = jnp.concatenate(mix, axis=0).T.astype(BF16)
         rows[...] = dot(pick, tok_all[k]).astype(BF16).reshape(per_dev, cap, features)
 
-    def stage_a(u):
-        i, e = u // per_dev, u % per_dev
-        turn = i // nz
-
-        @pl.when(u >= ring)
-        def _():
-            for r in crossing:
-                low_copy(u - ring, r).wait_send()
-
-        @pl.when(e == 0)
-        def _():
-            pick_rows(i)
-
+    def make_low(u):
+        e = u % per_dev
+        turn = u // per_dev // nz
         for h in range(2):
             weight = w1[turn, e, h * half : (h + 1) * half].reshape(half_width, dp * chunk)
             low = dot(rows[e, :, h * half_width : (h + 1) * half_width], weight).astype(BF16)
             for q in range(dp):
                 low_out[u % ring, q, h] = low[:, q * chunk : (q + 1) * chunk]
+
+    def send_low(u):
         for r in crossing:
             low_copy(u, r).start()
         low_local(u).start()
+
+    def stage_a(u):
+        @pl.when(u >= ring)
+        def _():
+            for r in crossing:
+                low_copy(u - ring, r).wait_send()
+
+        @pl.when(u % per_dev == 0)
+        def _():
+            meet(u // per_dev)
+            pick_rows(u // per_dev)
+
+        make_low(u)
+        send_low(u)
 
     def stage_b(u):
         i, e = u // per_dev, u % per_dev
@@ -473,6 +493,37 @@
 
     count_copy = remote(counts.at[1], counts_in, count_s.at[0], count_s.at[1], partner)
 
+    for n in range(5):
+        loads[n].wait()
+
+    @pl.when(inner)
+    def _():
+        pl.semaphore_wait(barrier, len(peers) + 1)
+
+    @pl.when(jnp.logical_not(inner))
+    def _():
+        pl.semaphore_wait(barrier, len(peers))
+
+    for h in range(2):
+        begin(gather(*sends[0], h))
+
+        @pl.when(inner)
+        def _():
+            begin(gather(*sends[1], h))
+
+    swap(0).start()
+    swap(1).start()
+    make_places()
+    pick_rows(0)
+
+    @pl.loop(0, per_dev)
+    def _(u):
+        spread_first(u, 0, gf, uf)
+        make_low(u)
+        send_low(u)
+
+    for n in range(5, len(loads)):
+        loads[n].wait()
     for e in range(per_dev):
         for c in range(rank_here):
             gs[e, c] = jnp.concatenate([gs_in[e, c], us_in[e, c]], axis=1)
@@ -487,16 +538,21 @@
         hit = (row3 >= offset) & (row3 < offset + block_count)
         place3[c] = one_hot(hit & (col3 == (row3 - offset) * rank_here + c))
 
+    @pl.loop(0, per_dev)
+    def _(u):
+        spread_middle(u, 0, gs, df)
+        stage_b(u)
+
+        @pl.when(u == per_dev - 2)
+        def _():
+            pass_tokens(0)
+
     far_steps = nz * per_dev
     first_at, middle_at = far_steps - per_dev - 1, far_steps + 1
     last_at = far_steps + lag_c
 
-    @pl.loop(0, units + lag_c)
+    @pl.loop(per_dev, units + lag_c)
     def _(t):
-        @pl.when(t < per_dev)
-        def _():
-            spread_first(t, 0, gf, uf)
-
         @pl.when((t >= first_at) & (t < first_at + per_dev))
         def _():
             @pl.when(t == first_at)
@@ -506,13 +562,13 @@
 
             spread_first(t - first_at, 1, gf2, uf2)
 
+        @pl.when(t == 2 * per_dev - 1)
+        def _():
+            pass_last(0)
+
         @pl.when(t < units)
         def _():
             stage_a(t)
-
-        @pl.when((t >= lag_b) & (t < lag_b + per_dev))
-        def _():
-            spread_middle(t - lag_b, 0, gs, df)
 
         @pl.when((t >= middle_at) & (t < middle_at + per_dev))
         def _():
@@ -523,7 +579,7 @@
 
             spread_middle(t - middle_at, 1, gs2, df2)
 
-        @pl.when((t >= lag_b) & (t < units + lag_b))
+        @pl.when((t >= lag_b + per_dev) & (t < units + lag_b))
         def _():
             stage_b(t - lag_b)
 
@@ -590,14 +646,15 @@
             z_wait(0, h)
             out[:, span] = (summed[0, h] + z_in[0, h].astype(F32)).astype(BF16)
 
-    for copy in sends[0]:
-        copy.wait_send()
-
-    @pl.when(inner)
-    def _():
-        for copies in (sends[1],) + relays:
-            for copy in copies:
-                copy.wait_send()
+    for h in range(2):
+        for copy in gather(*sends[0], h):
+            copy.wait_send()
+
+        @pl.when(inner)
+        def _():
+            for link in (sends[1],) + relays:
+                for copy in gather(*link, h):
+                    copy.wait_send()
 
     for n in range(3):
         for h in range(2):
@@ -638,7 +695,7 @@
     first = (per_dev, blocks, rank, width)
     joined = (per_dev, rank_here, block_count, 2 * block_count)
     paired = (per_dev, pairs, block_count, 2 * block_count)
-    last = down_second.shape
+    second, last = gate_second.shape, down_second.shape
     vmem = pl.BlockSpec(memory_space=pltpu.VMEM)
     dma = pltpu.SemaphoreType.DMA
     out, load = pl.pallas_call(
@@ -647,12 +704,13 @@
             jax.ShapeDtypeStruct((tok_rows, features), BF16),
             jax.ShapeDtypeStruct((1, per_dev), F32),
         ),
-        in_specs=[vmem] * 9,
+        in_specs=[pl.BlockSpec(memory_space=pl.ANY)] * 9,
         out_specs=(vmem, vmem),
         scratch_shapes=[
             pltpu.VMEM((nz, tok_rows, features), BF16),
             pltpu.VMEM((nz, top_k, tok_rows), jnp.int32),
             pltpu.VMEM((nz, top_k, tok_rows), F32),
+            *[pltpu.VMEM(s, BF16) for s in (first, first, second, second, second, last)],
             *[pltpu.VMEM(s, BF16) for s in (joined, paired)],
             *[pltpu.VMEM(s, BF16) for s in (first, first, joined, paired, last)],
             pltpu.VMEM((2, per_dev, blocks, width, dp * chunk), BF16),
@@ -673,9 +731,9 @@
             pltpu.VMEM((6, 2, tok_rows, half_width), BF16),
             pltpu.VMEM((2, 8, tok_rows), F32),
             pltpu.VMEM((8, tok_rows), F32),
-            dma((3, 5)), dma((3, nz)), dma((5,)), dma((5,)),
+            dma((4, 5)), dma((4, nz)), dma((5,)), dma((5,)),
             dma((ring, dp)), dma((units, dp)), dma((ring, dp)), dma((units, dp)),
-            dma((ring,)), dma((ring,)), dma((2,)), dma((3, 2)), dma((6, 2)),
+            dma((ring,)), dma((ring,)), dma((9,)), dma((2,)), dma((3, 2)), dma((6, 2)),
         ],
         compiler_params=pltpu.CompilerParams(
             collective_id=0, has_side_effects=True, vmem_limit_bytes=67043328

time: 106 us -> 101 us (0.953)
  Pallas kernels: 102 us -> 98.4 us
    pallas_call x1, Pallas kernels: 102 us -> 98.4 us  [fused(): pl.pallas_call(functools.partial(expert_kernel, (groups, dp, top_k, cap,...]
where the time goes in v2:
time: 101 us
  Pallas kernels  98.4 us (97%)
  local copies, waits for them, and re-layouts  2.33 us (2%)
    pallas_call x1, Pallas kernels, fused(): pl.pallas_call(functools.partial(expert_kernel, (groups, dp, top_k, cap,...  98.4 us
    unnamed x4, local copies, waits for them, and re-layouts  2.33 us

profile of v2, /device:TPU:0, one launch (start us, length us, event | category | flops | bytes accessed | tf_op | source)
XLA Modules:
  0.0 101.3 jit_solution(17263781127548074894)
XLA Ops:
  0.6 98.4 %shard_map.104 = (bf16[128,1792]{1,0:T(8,128)(2,1)}, f32[1,4]{1,0:T(1,128)}) custom-call(bf16[128,1792]{1,0:T(8,128)(2,1)} %tok.1, s32[8,128]{1,0:T(8,128)} %bitcast.7, f32[8,128]{1,0:T(8,128)} %bitcast.8, bf16[4,16,32,112]{3,2,1,0:T(8,128)(2,1)} %bitcast.5, bf16[4,16,32,112]{3,2,1,0:T(8,128)(2,1)} %bitcast.6, bf16[4,8,64,64]{3,2,1,0:T(8,128)(2,1)} %gs_arg.1, ...), custom_call_target="tpu_custom_call" | custom-call | tf_op jit(solution)/shard_map/pallas_call | solution.py:701
  99.0 0.0 copy-start
  99.0 1.8 %copy.13 = bf16[128,1792]{1,0:T(8,128)(2,1)} copy(bf16[128,1792]{1,0:T(8,128)(2,1)} %get-tuple-element.8) | data formatting | bytes 917504
  100.8 0.0 copy-done
  100.8 0.5 copy.14
Async XLA Ops:
  99.0 1.8 %copy-start = (f32[1,4]{1,0:T(1,128)S(1)}, f32[1,4]{1,0:T(1,128)}, u32[]{:S(2)}) copy-start(f32[1,4]{1,0:T(1,128)} %get-tuple-element.5) | copy-start | bytes 52

commit v3 on v2

--- a/solution.py
+++ b/solution.py
@@ -604,24 +604,29 @@
             count_copy.start()
 
         done_far = (steps - 2) * per_dev + lag_c - 1
-        for h in range(2):
-
-            @pl.when(inner & (t == done_far + h))
-            def _():
-                pass_far(h)
-
-        @pl.when(inner & (t == done_far + per_dev))
+        @pl.when(inner & (t == done_far + 0))
+        def _():
+            pass_far(0)
+
+        @pl.when(inner & (t == done_far + 1))
+        def _():
+            pass_far(1)
+
+        @pl.when(inner & (t == done_far + 5))
         def _():
             pass_across(0)
 
-        @pl.when(inner & (t == done_far + per_dev + 1))
+        @pl.when(inner & (t == done_far + 7))
+        def _():
+            pass_across(1)
+
+        @pl.when(inner & (t == done_far + 4))
         def _():
             pass_near(0)
 
-    @pl.when(inner)
-    def _():
-        pass_near(1)
-        pass_across(1)
+        @pl.when(inner & (t == done_far + 5))
+        def _():
+            pass_near(1)
 
     count_copy.wait()
     ones = jnp.ones((8, tok_rows), BF16)

time: 101 us -> 100 us (0.990)
  Pallas kernels: 98.4 us -> 96.7 us
    pallas_call x1, Pallas kernels: 98.4 us -> 96.7 us  [fused(): pl.pallas_call(functools.partial(expert_kernel, (groups, dp, top_k, cap,...]
where the time goes in v3:
time: 100 us; the launch traced here: 99.7 us
  Pallas kernels  96.7 us (97%)
  local copies, waits for them, and re-layouts  2.33 us (2%)
    pallas_call x1, Pallas kernels, fused(): pl.pallas_call(functools.partial(expert_kernel, (groups, dp, top_k, cap,...  96.7 us
    unnamed x4, local copies, waits for them, and re-layouts  2.33 us

profile of v3, /device:TPU:0, one launch (start us, length us, event | category | flops | bytes accessed | tf_op | source)
XLA Modules:
  0.0 99.7 jit_solution(1280788109193734170)
XLA Ops:
  0.6 96.7 %shard_map.104 = (bf16[128,1792]{1,0:T(8,128)(2,1)}, f32[1,4]{1,0:T(1,128)}) custom-call(bf16[128,1792]{1,0:T(8,128)(2,1)} %tok.1, s32[8,128]{1,0:T(8,128)} %bitcast.7, f32[8,128]{1,0:T(8,128)} %bitcast.8, bf16[4,16,32,112]{3,2,1,0:T(8,128)(2,1)} %bitcast.5, bf16[4,16,32,112]{3,2,1,0:T(8,128)(2,1)} %bitcast.6, bf16[4,8,64,64]{3,2,1,0:T(8,128)(2,1)} %gs_arg.1, ...), custom_call_target="tpu_custom_call" | custom-call | tf_op jit(solution)/shard_map/pallas_call | solution.py:706
  97.4 0.0 copy-start
  97.4 1.8 %copy.13 = bf16[128,1792]{1,0:T(8,128)(2,1)} copy(bf16[128,1792]{1,0:T(8,128)(2,1)} %get-tuple-element.8) | data formatting | bytes 917504
  99.2 0.0 copy-done
  99.2 0.5 copy.14
Async XLA Ops:
  97.4 1.8 %copy-start = (f32[1,4]{1,0:T(1,128)S(1)}, f32[1,4]{1,0:T(1,128)}, u32[]{:S(2)}) copy-start(f32[1,4]{1,0:T(1,128)} %get-tuple-element.5) | copy-start | bytes 52

commit v4 on v3

--- a/solution.py
+++ b/solution.py
@@ -612,7 +612,7 @@
         def _():
             pass_far(1)
 
-        @pl.when(inner & (t == done_far + 5))
+        @pl.when(inner & (t == done_far + 6))
         def _():
             pass_across(0)
 

time: 100 us -> 101 us (1.010)
  no operation moved by 1% of the time
where the time goes in v4:
time: 101 us; the launch traced here: 99.7 us
  Pallas kernels  96.7 us (96%)
  local copies, waits for them, and re-layouts  2.33 us (2%)
    pallas_call x1, Pallas kernels, fused(): pl.pallas_call(functools.partial(expert_kernel, (groups, dp, top_k, cap,...  96.7 us
    unnamed x4, local copies, waits for them, and re-layouts  2.33 us

profile of v4, /device:TPU:0, one launch (start us, length us, event | category | flops | bytes accessed | tf_op | source)
XLA Modules:
  0.0 99.7 jit_solution(6721264438793280032)
XLA Ops:
  0.6 96.7 %shard_map.104 = (bf16[128,1792]{1,0:T(8,128)(2,1)}, f32[1,4]{1,0:T(1,128)}) custom-call(bf16[128,1792]{1,0:T(8,128)(2,1)} %tok.1, s32[8,128]{1,0:T(8,128)} %bitcast.7, f32[8,128]{1,0:T(8,128)} %bitcast.8, bf16[4,16,32,112]{3,2,1,0:T(8,128)(2,1)} %bitcast.5, bf16[4,16,32,112]{3,2,1,0:T(8,128)(2,1)} %bitcast.6, bf16[4,8,64,64]{3,2,1,0:T(8,128)(2,1)} %gs_arg.1, ...), custom_call_target="tpu_custom_call" | custom-call | tf_op jit(solution)/shard_map/pallas_call | solution.py:706
  97.4 0.0 copy-start
  97.4 1.8 %copy.13 = bf16[128,1792]{1,0:T(8,128)(2,1)} copy(bf16[128,1792]{1,0:T(8,128)(2,1)} %get-tuple-element.8) | data formatting | bytes 917504
  99.2 0.0 copy-done
  99.2 0.5 copy.14
Async XLA Ops:
  97.4 1.8 %copy-start = (f32[1,4]{1,0:T(1,128)S(1)}, f32[1,4]{1,0:T(1,128)}, u32[]{:S(2)}) copy-start(f32[1,4]{1,0:T(1,128)} %get-tuple-element.5) | copy-start | bytes 52
